TPU v7x, 128 devices: a whole 4x4x4 slice. The times are simulated.
128 devices in a mesh: grp: 8 (over z, core), sub: 16 (over x, y).
Axes of the slice: x: 4, y: 4, z: 4, core: 2. Of those that a mesh axis runs over, the one named last changes fastest.
Arguments:
- rhs: float32 [96, 131072], P(None, ('grp', 'sub')), may hold values from -13 to 13
- blocks: bfloat16 [16384, 6656], P(('grp', 'sub')), may hold values from -0.05 to 0.45, as said below
- owners: int32 [16384, 1], P(('grp', 'sub')), may hold values from 0 to 7; in each aligned block of 128 rows (0 to 127, 128 to 255, ...) at most 48 rows name the same one
- conn: int32 [16384, 27], P(('grp', 'sub')), may hold values from 0 to 16383, as said below
Outputs:
- solution: float32 [96, 131072], P(None, ('grp', 'sub'))
- residual: float32 [96, 131072], P(None, ('grp', 'sub'))
Inputs may be any that keep to these rules, and one draw needn't show every extreme that they name: `blocks`: entries at positions 6561 and beyond are zero. `owners`: in each device's 128 rows at most 48 name the same column. `conn`: A column's nodes form layers of 128 nodes, node n in layer n // 128. An element in the rows of the device at position s along sub touches three consecutive layers, all within nodes s * 1024 to (s + 1) * 1024 + 2 * 128 - 1 of its column (within the column).
All inputs are finite; a program needn't handle non-finite values.
Results may differ from a plain program's by a relative error of at most 0.0075.
Values may be sent and summed in bfloat16 or wider, within the bound.
A program may use at most 192 MiB of HBM per device.

v0:
```python
import jax
import jax.numpy as jnp
from jax import lax
from jax.sharding import PartitionSpec as P

STEPS = 2
epsilon = 1e-06


def passed_along(block, axis, distance):
    devices = range(lax.axis_size(axis))
    route = [(i - distance, i) for i in devices if i - distance in devices]
    return lax.ppermute(block, axis, route)


def place_blocks(blocks, owners, conn, groups, capacity):
    owner_group = owners[:, 0]
    onehot = (owner_group[:, None] == jnp.arange(groups, dtype=jnp.int32)[None, :]).astype(
        jnp.int32
    )
    before = jnp.cumsum(onehot, axis=0) - onehot
    position = jnp.sum(before * onehot, axis=1)
    target = owner_group * capacity + position
    send_blocks = (
        jnp.zeros((groups * capacity, blocks.shape[1]), blocks.dtype).at[target].set(blocks)
    )
    send_links = jnp.zeros((groups * capacity, conn.shape[1]), jnp.int32).at[target].set(conn)
    return (send_blocks.reshape(groups, capacity, -1), send_links.reshape(groups, capacity, -1))


def window_product(matrix_groups, link_groups, field):
    rows = field.shape[0]
    window = field.shape[1]
    places = jnp.arange(window, dtype=jnp.int32)

    def one_group(acc, pair):
        matrix, links = pair
        slot_count = matrix.shape[0]
        selector = (links[:, None] == places[None, :]).astype(jnp.bfloat16)
        picked = jnp.einsum(
            "rw,lw->rl", field, selector, preferred_element_type=jnp.float32
        ).astype(jnp.bfloat16)
        picked = picked.reshape(3, rows // 3, slot_count, 27)
        result = jnp.einsum("spcqd,cosp->dosq", matrix, picked, preferred_element_type=jnp.float32)
        result = result.reshape(rows, slot_count * 27)
        high_part = result.astype(jnp.bfloat16)
        low_part = (result - high_part.astype(jnp.float32)).astype(jnp.bfloat16)
        acc = acc + jnp.dot(high_part, selector, preferred_element_type=jnp.float32)
        acc = acc + jnp.dot(low_part, selector, preferred_element_type=jnp.float32)
        return (acc, None)

    start = jnp.zeros((rows, window), jnp.float32)
    acc, unused = lax.scan(one_group, start, (matrix_groups, link_groups))
    return acc


def column_sums(first, second):
    return jnp.sum((first * second).reshape(3, -1, first.shape[1]), axis=(0, 2))


def update(solution, residual, image, along, energy):
    alpha = along / (energy + epsilon)
    scale_rows = jnp.tile(alpha, 3)[:, None]
    return (solution + scale_rows * residual, residual - scale_rows * image)


def shards(rhs, blocks, owners, conn):
    groups = lax.axis_size("grp")
    held = blocks.shape[0]
    capacity = max(2, 3 * held // 8)
    send_blocks, send_links = place_blocks(blocks, owners, conn, groups, capacity)
    got_blocks, got_links = (
        lax.all_to_all(send_blocks, "grp", split_axis=0, concat_axis=0, tiled=True),
        lax.all_to_all(send_links, "grp", split_axis=0, concat_axis=0, tiled=True),
    )
    matrix_groups = got_blocks[:, :, :6561].reshape(groups, capacity, 27, 3, 27, 3)
    residual = rhs
    solution = jnp.zeros(rhs.shape, jnp.float32)
    own_count = rhs.shape[1]
    band_width = 2 * held
    local_links = jnp.clip(
        got_links - lax.axis_index("sub") * own_count, 0, own_count + band_width - 1
    ).astype(jnp.int32)
    link_groups = local_links.reshape(groups, capacity * 27)
    for step in range(STEPS):
        rounded = residual.astype(jnp.bfloat16)
        upper = passed_along(rounded[:, :band_width], "sub", -1)
        field = jnp.concatenate([rounded, upper], axis=1)
        partial_sum = window_product(matrix_groups, link_groups, field)
        incoming = passed_along(partial_sum[:, own_count:], "sub", 1)
        image = partial_sum[:, :own_count] + jnp.pad(
            incoming, ((0, 0), (0, own_count - band_width))
        )
        along, energy = lax.psum(
            (column_sums(residual, image), column_sums(image, image)), ("grp", "sub")
        )
        solution, residual = update(solution, residual, image, along, energy)
    return (solution, residual)


def solution(mesh):
    return jax.shard_map(
        shards,
        mesh=mesh,
        in_specs=(
            P(None, ("grp", "sub")),
            P(("grp", "sub"), None),
            P(("grp", "sub"), None),
            P(("grp", "sub"), None),
        ),
        out_specs=(P(None, ("grp", "sub")), P(None, ("grp", "sub"))),
        check_vma=False,
    )
```

profile of v0, /device:TPU:1, one launch (start us, length us, event | category | flops | bytes accessed | tf_op | source)
XLA Modules:
  0.0 515.8 jit_solution(13757841406392980905)
XLA Ops:
  5.7 6.8 %all-to-all-start = ((s32[8,1,1296]{2,1,0:T(1,128)}), s32[8,1,1296]{2,1,0:T(1,128)S(1)}, u32[]{:S(2)}, u32[]{:S(2)}) async-start(s32[8,1,1296]{2,1,0:T(1,128)} %reshape.81), calls=%async_computation | async-start | bytes 90112 | tf_op jit(solution)/shard_map/all_to_all | solution.py:74
  12.5 6.9 %scatter_custom_fusion.1 = bf16[384,6656]{1,0:T(8,128)(2,1)} fusion(s32[128]{0:T(128)S(1)} %fusion.50, bf16[128,6656]{1,0:T(8,128)(2,1)} %param.9, bf16[]{:T(256)} %constant.23.clone.1), kind=kCustom, calls=%fused_computation.46 | custom fusion | bytes 5112320 | tf_op jit(solution)/shard_map/scatter | solution.py:25
  19.5 4.9 all-to-all-start.1
  29.8 53.3 %all-to-all-done.1 = bf16[8,48,6656]{2,1,0:T(8,128)(2,1)} async-done(((bf16[8,48,6656]{2,1,0:T(8,128)(2,1)}), bf16[8,48,6656]{2,1,0:T(8,128)(2,1)}, u32[]{:S(2)}, u32[]{:S(2)}) %all-to-all-start.1) | async-done | bytes 5111840 | tf_op jit(solution)/shard_map/all_to_all | solution.py:73
  83.1 14.8 %copy.45 = bf16[8,48,6561]{1,0,2:T(8,128)(2,1)} copy(bf16[8,48,6561]{2,1,0:T(8,128)(2,1)} %bitcast.44) | data formatting | bytes 10077696
  97.9 35.7 %copy.35 = bf16[8,48,27,3,27,3]{4,2,3,5,1,0:T(8,128)(2,1)} copy(bf16[8,48,27,3,27,3]{1,0,5,4,3,2:T(8,128)(2,1)} %bitcast.67) | data formatting | bytes 10077696
  133.6 112.3 %while.22 = (s32[]{:T(128)}, f32[96,1280]{1,0:T(8,128)}, s32[8,1296]{1,0:T(8,128)}, bf16[96,1280]{1,0:T(8,128)(2,1)S(1)}, bf16[8,48,27,3,27,3]{4,2,3,5,1,0:T(8,128)(2,1)}, /*index=5*/s32[]{:T(128)}, s32[]{:T(128)}) while((s32[]{:T(128)}, f32[96,1280]{1,0:T(8,128)}, s32[8,1296]{1,0:T(8,128)}, bf16[96,1280]{1,0:T(8,128)(2,1)S(1)}, ...), condition=%wide.region_5.6_spmd.clone, body=%wide.region_4.5_spmd.clone.sunk | while | flops 981762048 | bytes 10256283 | solution.py:53
  136.0 1.6 reshape.87
  137.7 2.8 fusion.75
  144.4 2.3 fusion.77
  150.8 2.8 fusion.75
  156.0 2.6 fusion.76
  158.6 2.3 fusion.77
  163.3 1.6 reshape.87
  165.0 2.8 fusion.75
  170.2 2.6 fusion.76
  172.8 2.3 fusion.77
  179.1 2.8 fusion.75
  184.3 2.6 fusion.76
  186.9 2.3 fusion.77
  191.6 1.6 reshape.87
  193.3 2.8 fusion.75
  198.5 2.6 fusion.76
  201.1 2.3 fusion.77
  207.5 2.8 fusion.75
  212.7 2.6 fusion.76
  215.3 2.3 fusion.77
  221.6 2.8 fusion.75
  226.8 2.6 fusion.76
  229.4 2.3 fusion.77
  235.8 2.8 fusion.75
  241.0 2.6 fusion.76
  243.6 2.3 fusion.77
  246.8 3.2 collective-permute-start.1
  253.0 66.9 %all-reduce.3 = (f32[32]{0:T(128)S(1)}, f32[32]{0:T(128)S(1)}) all-reduce(f32[32]{0:T(128)S(1)} %reduce_sum.62, f32[32]{0:T(128)S(1)} %reduce_sum.82), channel_id=1, replica_groups=mesh['grp'=8,'sub'=16] {'grp','sub'}, use_global_device_ids=true, to_apply=%region_8.9 | all-reduce | flops 64 | bytes 512 | tf_op jit(solution)/shard_map/psum | solution.py:94
  320.0 1.9 fusion.51
  323.4 3.3 collective-permute-done.2
  326.7 112.3 %while.23 = (s32[]{:T(128)}, f32[96,1280]{1,0:T(8,128)}, s32[8,1296]{1,0:T(8,128)}, bf16[96,1280]{1,0:T(8,128)(2,1)S(1)}, bf16[8,48,27,3,27,3]{4,2,3,5,1,0:T(8,128)(2,1)}, /*index=5*/s32[]{:T(128)}, s32[]{:T(128)}) while((s32[]{:T(128)}, f32[96,1280]{1,0:T(8,128)}, s32[8,1296]{1,0:T(8,128)}, bf16[96,1280]{1,0:T(8,128)(2,1)S(1)}, ...), condition=%wide.region_13.14_spmd.clone, body=%wide.region_12.13_spmd.clone.sunk | while | flops 981762048 | bytes 10256283 | solution.py:53
  330.8 2.8 fusion.83
  337.6 2.3 fusion.85
  343.9 2.8 fusion.83
  349.1 2.6 fusion.84
  351.7 2.3 fusion.85
  358.1 2.8 fusion.83
  363.3 2.6 fusion.84
  365.9 2.3 fusion.85
  372.3 2.8 fusion.83
  377.5 2.6 fusion.84
  380.0 2.3 fusion.85
  386.4 2.8 fusion.83
  391.6 2.6 fusion.84
  394.2 2.3 fusion.85
  400.6 2.8 fusion.83
  405.8 2.6 fusion.84
  408.4 2.3 fusion.85
  414.7 2.8 fusion.83
  419.9 2.6 fusion.84
  422.5 2.3 fusion.85
  428.9 2.8 fusion.83
  434.1 2.6 fusion.84
  436.7 2.3 fusion.85
  439.9 2.5 collective-permute-start.3
  445.6 68.0 %all-reduce.2 = (f32[32]{0:T(128)S(1)}, f32[32]{0:T(128)S(1)}) all-reduce(f32[32]{0:T(128)S(1)} %reduce_sum.85, f32[32]{0:T(128)S(1)} %reduce_sum.88), channel_id=1, replica_groups=mesh['grp'=8,'sub'=16] {'grp','sub'}, use_global_device_ids=true, to_apply=%region_16.17 | all-reduce | flops 64 | bytes 512 | tf_op jit(solution)/shard_map/psum | solution.py:94
  513.6 2.1 multiply_subtract_fusion
  (126 shorter events, 120.8 us)
Async XLA Ops:
  5.7 13.8 %all-to-all-start = ((s32[8,1,1296]{2,1,0:T(1,128)}), s32[8,1,1296]{2,1,0:T(1,128)S(1)}, u32[]{:S(2)}, u32[]{:S(2)}) async-start(s32[8,1,1296]{2,1,0:T(1,128)} %reshape.81), calls=%async_computation | async-start | bytes 90112 | tf_op jit(solution)/shard_map/all_to_all | solution.py:74
  19.5 4.9 copy-start
  19.5 63.7 %all-to-all-start.1 = ((bf16[8,48,6656]{2,1,0:T(8,128)(2,1)}), bf16[8,48,6656]{2,1,0:T(8,128)(2,1)}, u32[]{:S(2)}, u32[]{:S(2)}) async-start(bf16[8,48,6656]{2,1,0:T(8,128)(2,1)} %bitcast.68), calls=%async_computation.1 | async-start | bytes 10223616 | tf_op jit(solution)/shard_map/all_to_all | solution.py:73
  24.4 5.4 %collective-permute-start = (bf16[96,256]{1,0:T(8,128)(2,1)S(1)}, bf16[96,256]{1,0:T(8,128)(2,1)S(1)}, u32[]{:S(2)}, u32[]{:S(2)}) collective-permute-start(bf16[96,256]{1,0:T(8,128)(2,1)S(1)} %slice.28), channel_id=1, source_target_pairs={{1,0},{2,1},{3,2},{4,3},{5,4},{6,5},{7,6},{8,7},{9,8},{10,9},{11,1... | collective-permute-start | bytes 147464 | tf_op jit(solution)/shard_map/ppermute | solution.py:13
  246.8 4.8 collective-permute-start.1
  321.9 4.8 collective-permute-start.2
  439.9 4.1 collective-permute-start.3
where the time goes:
time: 520 us; the launch traced here: 516 us
  matrix products  147 us (28%)
  local copies, waits for them, and re-layouts  141 us (27%)
  blocking collectives  135 us (26%)
  waiting for transfers between devices  61.3 us (12%)
  starting transfers between devices  20.5 us (4%)
  other arithmetic  9.82 us (2%)
    psum x2, blocking collectives, shards(): lax.psum((column_sums(residual, image), column_sums(image, image)), ('grp...  135 us
    all_to_all x1, waiting for transfers between devices, shards(): lax.all_to_all(send_blocks, 'grp', split_axis=0, concat_axis=0, tiled=True)  53.3 us
    unnamed x7, local copies, waits for them, and re-layouts  52.2 us
    dot_general x16, matrix products, one_group(): jnp.einsum('spcqd,cosp->dosq', matrix, picked, preferred_element_type=jnp...  44.9 us
    dot_general x16, matrix products, one_group(): acc = acc + jnp.dot(high_part, selector, preferred_element_type=jnp.float32)  39.2 us
    dot_general x16, matrix products, one_group(): acc = acc + jnp.dot(low_part, selector, preferred_element_type=jnp.float32)  37.2 us
    reshape x16, local copies, waits for them, and re-layouts, one_group(): picked = picked.reshape(3, rows // 3, slot_count, 27)  26.4 us
    dot_general x16, matrix products, one_group(): jnp.einsum('rw,lw->rl', field, selector, preferred_element_type=jnp.float32)  25.1 us
  transfers between devices with their start and end apart: 6, of which 5 were waited for; matrix products, arithmetic and copies ran while one was open for 2% of the time, Pallas kernels for 0%

commit v1 on v0

--- a/solution.py
+++ b/solution.py
@@ -91,9 +91,13 @@
         image = partial_sum[:, :own_count] + jnp.pad(
             incoming, ((0, 0), (0, own_count - band_width))
         )
-        along, energy = lax.psum(
-            (column_sums(residual, image), column_sums(image, image)), ("grp", "sub")
-        )
+
+        def obtain_things(slab_in):
+            mixed_arr = lax.psum(slab_in, "grp")
+            t_next = lax.psum(mixed_arr, "sub")
+            return t_next
+
+        along, energy = obtain_things((column_sums(residual, image), column_sums(image, image)))
         solution, residual = update(solution, residual, image, along, energy)
     return (solution, residual)
 

time: 520 us -> 490 us (0.942)
  the two profiles are of different devices: /device:TPU:1 before, /device:TPU:0 now
where the time goes in v1:
time: 490 us; the launch traced here: 486 us
  matrix products  147 us (30%)
  local copies, waits for them, and re-layouts  141 us (29%)
  blocking collectives  104 us (21%)
  waiting for transfers between devices  64.5 us (13%)
  starting transfers between devices  18.4 us (4%)
  other arithmetic  9.83 us (2%)
    psum x2, blocking collectives, obtain_things(): t_next = lax.psum(mixed_arr, 'sub')  79.3 us
    all_to_all x1, waiting for transfers between devices, shards(): lax.all_to_all(send_blocks, 'grp', split_axis=0, concat_axis=0, tiled=True)  53.5 us
    unnamed x7, local copies, waits for them, and re-layouts  52.2 us
    dot_general x16, matrix products, one_group(): jnp.einsum('spcqd,cosp->dosq', matrix, picked, preferred_element_type=jnp...  44.9 us
    dot_general x16, matrix products, one_group(): acc = acc + jnp.dot(high_part, selector, preferred_element_type=jnp.float32)  39.2 us
    dot_general x16, matrix products, one_group(): acc = acc + jnp.dot(low_part, selector, preferred_element_type=jnp.float32)  37.2 us
    reshape x16, local copies, waits for them, and re-layouts, one_group(): picked = picked.reshape(3, rows // 3, slot_count, 27)  26.4 us
    dot_general x16, matrix products, one_group(): jnp.einsum('rw,lw->rl', field, selector, preferred_element_type=jnp.float32)  25.1 us
  transfers between devices with their start and end apart: 6, of which 5 were waited for; matrix products, arithmetic and copies ran while one was open for 2% of the time, Pallas kernels for 0%

profile of v1, /device:TPU:0, one launch (start us, length us, event | category | flops | bytes accessed | tf_op | source)
XLA Modules:
  0.0 486.1 jit_solution(8484267942732070464)
XLA Ops:
  5.7 5.4 %all-to-all-start = ((s32[8,1,1296]{2,1,0:T(1,128)}), s32[8,1,1296]{2,1,0:T(1,128)S(1)}, u32[]{:S(2)}, u32[]{:S(2)}) async-start(s32[8,1,1296]{2,1,0:T(1,128)} %reshape.81), calls=%async_computation | async-start | bytes 90112 | tf_op jit(solution)/shard_map/all_to_all | solution.py:74
  11.1 6.9 %scatter_custom_fusion.1 = bf16[384,6656]{1,0:T(8,128)(2,1)} fusion(s32[128]{0:T(128)S(1)} %fusion.50, bf16[128,6656]{1,0:T(8,128)(2,1)} %param.9, bf16[]{:T(256)} %constant.23.clone.1), kind=kCustom, calls=%fused_computation.46 | custom fusion | bytes 5112320 | tf_op jit(solution)/shard_map/scatter | solution.py:25
  18.1 4.9 %all-to-all-start.1 = ((bf16[8,48,6656]{2,1,0:T(8,128)(2,1)}), bf16[8,48,6656]{2,1,0:T(8,128)(2,1)}, u32[]{:S(2)}, u32[]{:S(2)}) async-start(bf16[8,48,6656]{2,1,0:T(8,128)(2,1)} %bitcast.68), calls=%async_computation.1 | async-start | bytes 10223616 | tf_op jit(solution)/shard_map/all_to_all | solution.py:73
  26.9 2.2 collective-permute-done
  29.1 53.5 %all-to-all-done.1 = bf16[8,48,6656]{2,1,0:T(8,128)(2,1)} async-done(((bf16[8,48,6656]{2,1,0:T(8,128)(2,1)}), bf16[8,48,6656]{2,1,0:T(8,128)(2,1)}, u32[]{:S(2)}, u32[]{:S(2)}) %all-to-all-start.1) | async-done | bytes 5111840 | tf_op jit(solution)/shard_map/all_to_all | solution.py:73
  82.6 14.8 %copy.45 = bf16[8,48,6561]{1,0,2:T(8,128)(2,1)} copy(bf16[8,48,6561]{2,1,0:T(8,128)(2,1)} %bitcast.44) | data formatting | bytes 10077696
  97.4 35.7 %copy.35 = bf16[8,48,27,3,27,3]{4,2,3,5,1,0:T(8,128)(2,1)} copy(bf16[8,48,27,3,27,3]{1,0,5,4,3,2:T(8,128)(2,1)} %bitcast.67) | data formatting | bytes 10077696
  133.1 112.3 %while.22 = (s32[]{:T(128)}, f32[96,1280]{1,0:T(8,128)}, s32[8,1296]{1,0:T(8,128)}, bf16[96,1280]{1,0:T(8,128)(2,1)S(1)}, bf16[8,48,27,3,27,3]{4,2,3,5,1,0:T(8,128)(2,1)}, /*index=5*/s32[]{:T(128)}, s32[]{:T(128)}) while((s32[]{:T(128)}, f32[96,1280]{1,0:T(8,128)}, s32[8,1296]{1,0:T(8,128)}, bf16[96,1280]{1,0:T(8,128)(2,1)S(1)}, ...), condition=%wide.region_5.6_spmd.clone, body=%wide.region_4.5_spmd.clone.sunk | while | flops 981762048 | bytes 10256283 | solution.py:53
  137.1 2.8 fusion.75
  143.9 2.3 fusion.77
  150.3 2.8 fusion.75
  155.5 2.6 fusion.76
  158.0 2.3 fusion.77
  164.4 2.8 fusion.75
  169.6 2.6 fusion.76
  172.2 2.3 fusion.77
  178.6 2.8 fusion.75
  183.8 2.6 fusion.76
  186.4 2.3 fusion.77
  192.7 2.8 fusion.75
  197.9 2.6 fusion.76
  200.5 2.3 fusion.77
  206.9 2.8 fusion.75
  212.1 2.6 fusion.76
  214.7 2.3 fusion.77
  221.1 2.8 fusion.75
  226.3 2.6 fusion.76
  228.9 2.3 fusion.77
  235.2 2.8 fusion.75
  240.4 2.6 fusion.76
  243.0 2.3 fusion.77
  246.3 3.5 collective-permute-start.1
  249.7 2.2 collective-permute-done.1
  253.3 12.4 %all-reduce.5 = (f32[32]{0:T(128)S(1)}, f32[32]{0:T(128)S(1)}) all-reduce(f32[32]{0:T(128)S(1)} %reduce_sum.62, f32[32]{0:T(128)S(1)} %reduce_sum.82), channel_id=1, replica_groups=mesh['grp'=8,'sub'=16] {'grp'}, use_global_device_ids=true, to_apply=%region_8.9 | all-reduce | flops 64 | bytes 512 | tf_op jit(solution)/shard_map/psum | solution.py:96
  265.7 41.5 %all-reduce.3 = (f32[32]{0:T(128)S(1)}, f32[32]{0:T(128)S(1)}) all-reduce(f32[32]{0:T(128)S(1)} %get-tuple-element.168, f32[32]{0:T(128)S(1)} %get-tuple-element.169), channel_id=1, replica_groups=mesh['grp'=8,'sub'=16] {'sub'}, use_global_device_ids=true, to_apply=%region_9.10 | all-reduce | flops 64 | bytes 512 | tf_op jit(solution)/shard_map/psum | solution.py:97
  310.7 4.5 collective-permute-done.2
  315.2 112.3 %while.23 = (s32[]{:T(128)}, f32[96,1280]{1,0:T(8,128)}, s32[8,1296]{1,0:T(8,128)}, bf16[96,1280]{1,0:T(8,128)(2,1)S(1)}, bf16[8,48,27,3,27,3]{4,2,3,5,1,0:T(8,128)(2,1)}, /*index=5*/s32[]{:T(128)}, s32[]{:T(128)}) while((s32[]{:T(128)}, f32[96,1280]{1,0:T(8,128)}, s32[8,1296]{1,0:T(8,128)}, bf16[96,1280]{1,0:T(8,128)(2,1)S(1)}, ...), condition=%wide.region_15.16_spmd.clone, body=%wide.region_14.15_spmd.clone.sunk | while | flops 981762048 | bytes 10256283 | solution.py:53
  319.2 2.8 fusion.83
  326.0 2.3 fusion.85
  332.4 2.8 fusion.83
  337.6 2.6 fusion.84
  340.1 2.3 fusion.85
  346.5 2.8 fusion.83
  351.7 2.6 fusion.84
  354.3 2.3 fusion.85
  360.7 2.8 fusion.83
  365.9 2.6 fusion.84
  368.5 2.3 fusion.85
  374.8 2.8 fusion.83
  380.1 2.6 fusion.84
  382.6 2.3 fusion.85
  389.0 2.8 fusion.83
  394.2 2.6 fusion.84
  396.8 2.3 fusion.85
  403.2 2.8 fusion.83
  408.4 2.6 fusion.84
  411.0 2.3 fusion.85
  417.3 2.8 fusion.83
  422.5 2.6 fusion.84
  425.1 2.3 fusion.85
  430.0 2.2 collective-permute-done.3
  433.6 12.4 %all-reduce.4 = (f32[32]{0:T(128)S(1)}, f32[32]{0:T(128)S(1)}) all-reduce(f32[32]{0:T(128)S(1)} %reduce_sum.85, f32[32]{0:T(128)S(1)} %reduce_sum.88), channel_id=1, replica_groups=mesh['grp'=8,'sub'=16] {'grp'}, use_global_device_ids=true, to_apply=%region_18.19 | all-reduce | flops 64 | bytes 512 | tf_op jit(solution)/shard_map/psum | solution.py:96
  446.1 37.8 %all-reduce.2 = (f32[32]{0:T(128)S(1)}, f32[32]{0:T(128)S(1)}) all-reduce(f32[32]{0:T(128)S(1)} %get-tuple-element.166, f32[32]{0:T(128)S(1)} %get-tuple-element.167), channel_id=1, replica_groups=mesh['grp'=8,'sub'=16] {'sub'}, use_global_device_ids=true, to_apply=%region_19.20 | all-reduce | flops 64 | bytes 512 | tf_op jit(solution)/shard_map/psum | solution.py:97
  484.0 2.1 multiply_subtract_fusion
  (128 shorter events, 124.4 us)
Async XLA Ops:
  5.7 12.3 %all-to-all-start = ((s32[8,1,1296]{2,1,0:T(1,128)}), s32[8,1,1296]{2,1,0:T(1,128)S(1)}, u32[]{:S(2)}, u32[]{:S(2)}) async-start(s32[8,1,1296]{2,1,0:T(1,128)} %reshape.81), calls=%async_computation | async-start | bytes 90112 | tf_op jit(solution)/shard_map/all_to_all | solution.py:74
  18.0 4.9 %copy-start = (f32[96,1024]{1,0:T(8,128)S(1)}, f32[96,1024]{1,0:T(8,128)}, u32[]{:S(2)}) copy-start(f32[96,1024]{1,0:T(8,128)} %param.8) | copy-start | bytes 1179652
  18.1 64.5 %all-to-all-start.1 = ((bf16[8,48,6656]{2,1,0:T(8,128)(2,1)}), bf16[8,48,6656]{2,1,0:T(8,128)(2,1)}, u32[]{:S(2)}, u32[]{:S(2)}) async-start(bf16[8,48,6656]{2,1,0:T(8,128)(2,1)} %bitcast.68), calls=%async_computation.1 | async-start | bytes 10223616 | tf_op jit(solution)/shard_map/all_to_all | solution.py:73
  23.0 6.0 %collective-permute-start = (bf16[96,256]{1,0:T(8,128)(2,1)S(1)}, bf16[96,256]{1,0:T(8,128)(2,1)S(1)}, u32[]{:S(2)}, u32[]{:S(2)}) collective-permute-start(bf16[96,256]{1,0:T(8,128)(2,1)S(1)} %slice.28), channel_id=1, source_target_pairs={{1,0},{2,1},{3,2},{4,3},{5,4},{6,5},{7,6},{8,7},{9,8},{10,9},{11,1... | collective-permute-start | bytes 147464 | tf_op jit(solution)/shard_map/ppermute | solution.py:13
  246.3 5.7 %collective-permute-start.1 = (f32[96,256]{1,0:T(8,128)S(1)}, f32[96,256]{1,0:T(8,128)S(1)}, u32[]{:S(2)}, u32[]{:S(2)}) collective-permute-start(f32[96,256]{1,0:T(8,128)S(1)} %slice.24), channel_id=1, source_target_pairs={{0,1},{1,2},{2,3},{3,4},{4,5},{5,6},{6,7},{7,8},{8,9},{9,10},{10,1... | collective-permute-start | bytes 294920 | tf_op jit(solution)/shard_map/ppermute | solution.py:13
  309.2 6.0 %collective-permute-start.2 = (bf16[96,256]{1,0:T(8,128)(2,1)S(1)}, bf16[96,256]{1,0:T(8,128)(2,1)S(1)}, u32[]{:S(2)}, u32[]{:S(2)}) collective-permute-start(bf16[96,256]{1,0:T(8,128)(2,1)S(1)} %slice.30), channel_id=1, source_target_pairs={{1,0},{2,1},{3,2},{4,3},{5,4},{6,5},{7,6},{8,7},{9,8},{10,9},{11,1... | collective-permute-start | bytes 147464 | tf_op jit(solution)/shard_map/ppermute | solution.py:13
  428.4 3.8 collective-permute-start.3
